TPU v7x, 128 devices: a whole 4x4x4 slice. The times are simulated.
128 devices in a mesh: src: 16 (over x_lo, z, core), tgt: 8 (over y, x_hi).
Axes of the slice: x: 4 (x_hi: 2, x_lo: 2; x = x_hi * 2 + x_lo), y: 4, z: 4, core: 2. Of those that a mesh axis runs over, the one named last changes fastest.
Arguments:
- source_field: bfloat16 [1024, 1024, 256], P(None, ('src', 'tgt')), may hold values from -6 to 6
- self_weight: bfloat16 [4, 1024, 256, 256], P(None, ('src', 'tgt')), may hold values from -0.25 to 0.25
- cross_weight: bfloat16 [4, 1024, 256, 256], P(None, ('src', 'tgt')), may hold values from -0.25 to 0.25
- level_bias: float32 [4, 1024, 256], P(None, ('src', 'tgt')), may hold values from -3 to 3
- switch_weight: bfloat16 [1024, 256, 256], P(('src', 'tgt')), may hold values from -0.375 to 0.375
- switch_bias: float32 [1024, 256], P(('src', 'tgt')), may hold values from -3 to 3
Outputs:
- target_field: bfloat16 [1024, 1024, 256], P(None, ('src', 'tgt'))
All inputs are finite; a program needn't handle non-finite values.
Results may differ from a plain program's by a relative error of at most 0.0057.
Values may be sent and summed in bfloat16 or wider, within the bound.
A program may use at most 64 MiB of HBM per device.

v0:
```python
import jax
import jax.numpy as jnp
from jax import lax
from jax.sharding import PartitionSpec as P


def from_partner(value, axis, apart):
    return lax.ppermute(value, axis, [(i, i ^ 1 << apart) for i in range(lax.axis_size(axis))])


def level_step(field, self_w, cross_w, bias, bit_number):
    own_part = jnp.einsum("sbi,bio->sbo", field, self_w, preferred_element_type=jnp.float32)
    local_term = jnp.einsum(
        "sbi,bio->sbo", field, cross_w, preferred_element_type=jnp.float32
    ).astype(jnp.bfloat16)
    term = from_partner(local_term, "src", bit_number)
    term = lax.optimization_barrier(term)
    return jax.nn.relu(own_part + term.astype(jnp.float32) + bias[None]).astype(jnp.bfloat16)


def per_device(source_field, self_weight, cross_weight, level_bias, switch_weight, switch_bias):
    high_bit = lax.axis_size("src").bit_length() - 2
    bit_list = [0, high_bit, high_bit - 1, 1]
    field = source_field
    for layer_index in range(2):
        field = level_step(
            field,
            self_weight[layer_index],
            cross_weight[layer_index],
            level_bias[layer_index],
            bit_list[layer_index],
        )
    product = jnp.einsum(
        "sbi,bio->sbo",
        lax.all_to_all(field, "tgt", split_axis=2, concat_axis=2, tiled=True),
        switch_weight,
        preferred_element_type=jnp.float32,
    )
    field = jax.nn.relu(product + switch_bias[None]).astype(jnp.bfloat16)
    for layer_index in range(2, 4):
        field = level_step(
            field,
            self_weight[layer_index],
            cross_weight[layer_index],
            level_bias[layer_index],
            bit_list[layer_index],
        )
    return field


def solution(mesh):
    placed = (
        P(None, ("src", "tgt"), None),
        P(None, ("src", "tgt"), None, None),
        P(None, ("src", "tgt"), None, None),
        P(None, ("src", "tgt"), None),
        P(("src", "tgt"), None, None),
        P(("src", "tgt"), None),
    )
    return jax.shard_map(
        per_device,
        mesh=mesh,
        in_specs=placed,
        out_specs=P(None, ("src", "tgt"), None),
        check_vma=False,
    )
```

profile of v0, /device:TPU:0, one launch (start us, length us, event | category | flops | bytes accessed | tf_op | source)
XLA Modules:
  0.0 375.6 jit_solution(1674530343895179324)
XLA Ops:
  0.0 4.9 %convert_bitcast_fusion.3 = bf16[1024,8,256]{0,2,1:T(8,128)(2,1)S(1)} fusion(bf16[1024,8,256]{2,1,0:T(8,128)(2,1)} %param.6, bf16[4,8,256,256]{3,2,1,0:T(8,128)(2,1)} %param.8), kind=kOutput, calls=%fused_computation.23 | convolution fusion | flops 1075838976 | bytes 9437184 | tf_op jit(solution)/shard_map/sbi,bio->sbo/dot_general | solution.py:13
  4.9 0.1 collective-permute-start
  5.0 3.1 fusion.17
  8.1 4.0 %collective-permute-done = bf16[1024,8,256]{0,2,1:T(8,128)(2,1)S(1)} collective-permute-done((bf16[1024,8,256]{0,2,1:T(8,128)(2,1)S(1)}, bf16[1024,8,256]{0,2,1:T(8,128)(2,1)S(1)}, u32[]{:S(2)}, u32[]{:S(2)}) %collective-permute-start) | collective-permute-done | bytes 4194336 | tf_op jit(solution)/shard_map/ppermute | solution.py:8
  12.1 1.3 fusion.11
  13.4 0.9 copy-done.3
  14.3 1.3 convert_bitcast_fusion.2
  15.6 1.7 collective-permute-start.1
  17.3 91.0 %collective-permute-done.1 = bf16[1024,8,256]{0,2,1:T(8,128)(2,1)S(1)} collective-permute-done((bf16[1024,8,256]{0,2,1:T(8,128)(2,1)S(1)}, bf16[1024,8,256]{0,2,1:T(8,128)(2,1)S(1)}, u32[]{:S(2)}, u32[]{:S(2)}) %collective-permute-start.1) | collective-permute-done | bytes 4194336 | tf_op jit(solution)/shard_map/ppermute | solution.py:8
  108.3 3.3 fusion.8
  111.6 2.3 copy.23
  113.9 0.0 copy-start.5
  113.9 57.2 %all_to_all.5 = bf16[1024,8,256]{0,1,2:T(8,128)(2,1)S(1)} all-to-all(bf16[1024,8,256]{0,1,2:T(8,128)(2,1)S(1)} %copy.23), channel_id=1, replica_groups=mesh['src'=16,'tgt'=8] {'tgt'}, dimensions={2} | all-to-all | bytes 8388608 | tf_op jit(solution)/shard_map/all_to_all | solution.py:35
  171.1 5.3 %fusion.12 = bf16[1024,8,256]{2,0,1:T(8,128)(2,1)S(1)} fusion(f32[8,256]{1,0:T(8,128)S(1)} %copy-done.5, bf16[8,256,256]{2,1,0:T(8,128)(2,1)S(1)} %copy-done, bf16[1024,8,256]{0,1,2:T(8,128)(2,1)S(1)} %all_to_all.5), kind=kOutput, calls=%fused_computation.17 | convolution fusion | flops 1080033280 | bytes 9445376 | tf_op jit(solution)/shard_map/sbi,bio->sbo/dot_general | solution.py:33
  176.4 1.3 convert_bitcast_fusion.1
  177.7 3.9 %collective-permute-start.2 = (bf16[1024,8,256]{0,2,1:T(8,128)(2,1)S(1)}, bf16[1024,8,256]{0,2,1:T(8,128)(2,1)S(1)}, u32[]{:S(2)}, u32[]{:S(2)}) collective-permute-start(bf16[1024,8,256]{0,2,1:T(8,128)(2,1)S(1)} %convert_bitcast_fusion.1), channel_id=1, source_target_pairs={{0,32},{8,40},{16,48},{24,56},{32,0},{40,8},{48,16},{56,24},{64,96... | collective-permute-start | bytes 12582920 | tf_op jit(solution)/shard_map/ppermute | solution.py:8
  181.7 2.5 fusion.28
  184.2 86.3 %collective-permute-done.2 = bf16[1024,8,256]{0,2,1:T(8,128)(2,1)S(1)} collective-permute-done((bf16[1024,8,256]{0,2,1:T(8,128)(2,1)S(1)}, bf16[1024,8,256]{0,2,1:T(8,128)(2,1)S(1)}, u32[]{:S(2)}, u32[]{:S(2)}) %collective-permute-start.2) | collective-permute-done | bytes 4194336 | tf_op jit(solution)/shard_map/ppermute | solution.py:8
  270.6 1.4 fusion.5
  272.0 1.3 convert_bitcast_fusion
  273.3 1.4 collective-permute-start.3
  274.7 88.7 %collective-permute-done.3 = bf16[1024,8,256]{0,2,1:T(8,128)(2,1)S(1)} collective-permute-done((bf16[1024,8,256]{0,2,1:T(8,128)(2,1)S(1)}, bf16[1024,8,256]{0,2,1:T(8,128)(2,1)S(1)}, u32[]{:S(2)}, u32[]{:S(2)}) %collective-permute-start.3) | collective-permute-done | bytes 4194336 | tf_op jit(solution)/shard_map/ppermute | solution.py:8
  363.4 5.3 %fusion.2 = bf16[1024,8,256]{0,2,1:T(8,128)(2,1)} fusion(bf16[1024,8,256]{0,2,1:T(8,128)(2,1)S(1)} %collective-permute-done.3, f32[8,256]{1,0:T(8,128)S(1)} %get-tuple-element.5, bf16[1024,8,256]{0,2,1:T(8,128)(2,1)S(1)} %fusion.5, bf16[4,8,256,256]{3,2,1,0:T(8,128)(2,1)} %param.7), kind=kOutput, calls=%fused_computation.3 | convolution fusion | flops 1084227584 | bytes 13639680 | tf_op jit(solution)/shard_map/sbi,bio->sbo/dot_general | solution.py:12
  368.7 6.9 %copy.31 = bf16[1024,8,256]{2,1,0:T(8,128)(2,1)} copy(bf16[1024,8,256]{0,2,1:T(8,128)(2,1)} %fusion.2) | data formatting | bytes 8388608 | tf_op jit(solution)/shard_map/convert_element_type | solution.py:18
  (11 shorter events, 0.0 us)
Async XLA Ops:
  0.0 171.1 %copy-start = (bf16[8,256,256]{2,1,0:T(8,128)(2,1)S(1)}, bf16[8,256,256]{2,1,0:T(8,128)(2,1)}, u32[]{:S(2)}) copy-start(bf16[8,256,256]{2,1,0:T(8,128)(2,1)} %param.10) | copy-start | bytes 3145732
  0.0 5.0 %copy-start.2 = (bf16[1024,8,256]{2,1,0:T(8,128)(2,1)S(1)}, bf16[1024,8,256]{2,1,0:T(8,128)(2,1)}, u32[]{:S(2)}) copy-start(bf16[1024,8,256]{2,1,0:T(8,128)(2,1)} %param.6) | copy-start | bytes 12582916
  0.0 5.0 %copy-start.4 = (f32[4,8,256]{2,1,0:T(8,128)S(1)}, f32[4,8,256]{2,1,0:T(8,128)}, u32[]{:S(2)}) copy-start(f32[4,8,256]{2,1,0:T(8,128)} %param.9) | copy-start | bytes 98308
  4.9 7.2 %collective-permute-start = (bf16[1024,8,256]{0,2,1:T(8,128)(2,1)S(1)}, bf16[1024,8,256]{0,2,1:T(8,128)(2,1)S(1)}, u32[]{:S(2)}, u32[]{:S(2)}) collective-permute-start(bf16[1024,8,256]{0,2,1:T(8,128)(2,1)S(1)} %convert_bitcast_fusion.3), channel_id=1, source_target_pairs={{0,8},{8,0},{16,24},{24,16},{32,40},{40,32},{48,56},{56,48},{64,72... | collective-permute-start | bytes 12582920 | tf_op jit(solution)/shard_map/ppermute | solution.py:8
  12.1 2.2 copy-start.3
  15.6 92.7 %collective-permute-start.1 = (bf16[1024,8,256]{0,2,1:T(8,128)(2,1)S(1)}, bf16[1024,8,256]{0,2,1:T(8,128)(2,1)S(1)}, u32[]{:S(2)}, u32[]{:S(2)}) collective-permute-start(bf16[1024,8,256]{0,2,1:T(8,128)(2,1)S(1)} %convert_bitcast_fusion.2), channel_id=1, source_target_pairs={{0,64},{8,72},{16,80},{24,88},{32,96},{40,104},{48,112},{56,120},{... | collective-permute-start | bytes 12582920 | tf_op jit(solution)/shard_map/ppermute | solution.py:8
  113.9 57.2 %copy-start.5 = (f32[8,256]{1,0:T(8,128)S(1)}, f32[8,256]{1,0:T(8,128)}, u32[]{:S(2)}) copy-start(f32[8,256]{1,0:T(8,128)} %param.11) | copy-start | bytes 24580
  177.7 92.8 %collective-permute-start.2 = (bf16[1024,8,256]{0,2,1:T(8,128)(2,1)S(1)}, bf16[1024,8,256]{0,2,1:T(8,128)(2,1)S(1)}, u32[]{:S(2)}, u32[]{:S(2)}) collective-permute-start(bf16[1024,8,256]{0,2,1:T(8,128)(2,1)S(1)} %convert_bitcast_fusion.1), channel_id=1, source_target_pairs={{0,32},{8,40},{16,48},{24,56},{32,0},{40,8},{48,16},{56,24},{64,96... | collective-permute-start | bytes 12582920 | tf_op jit(solution)/shard_map/ppermute | solution.py:8
  273.3 90.1 %collective-permute-start.3 = (bf16[1024,8,256]{0,2,1:T(8,128)(2,1)S(1)}, bf16[1024,8,256]{0,2,1:T(8,128)(2,1)S(1)}, u32[]{:S(2)}, u32[]{:S(2)}) collective-permute-start(bf16[1024,8,256]{0,2,1:T(8,128)(2,1)S(1)} %convert_bitcast_fusion), channel_id=1, source_target_pairs={{0,16},{8,24},{16,0},{24,8},{32,48},{40,56},{48,32},{56,40},{64,80... | collective-permute-start | bytes 12582920 | tf_op jit(solution)/shard_map/ppermute | solution.py:8
  363.4 12.2 %copy-start.1 = (bf16[8,256,256]{2,1,0:T(8,128)(2,1)S(1)}, bf16[8,256,256]{2,1,0:T(8,128)(2,1)}, u32[]{:S(2)}) copy-start(bf16[8,256,256]{2,1,0:T(8,128)(2,1)} %param.10) | copy-start | bytes 3145732
where the time goes:
time: 376 us
  waiting for transfers between devices  270 us (72%)
  blocking collectives  57.2 us (15%)
  matrix products  28.3 us (8%)
  local copies, waits for them, and re-layouts  10.1 us (3%)
  starting transfers between devices  7.12 us (2%)
    ppermute x4, waiting for transfers between devices, from_partner(): lax.ppermute(value, axis, [(i, i ^ 1 << apart) for i in range(lax.axis_si...  270 us
    all_to_all x1, blocking collectives, per_device(): lax.all_to_all(field, 'tgt', split_axis=2, concat_axis=2, tiled=True)  57.2 us
    dot_general x4, matrix products, level_step(): jnp.einsum('sbi,bio->sbo', field, self_w, preferred_element_type=jnp.floa...  14.2 us
    convert_element_type x2, local copies, waits for them, and re-layouts, level_step(): jax.nn.relu(own_part + term.astype(jnp.float32) + bias[None])  9.19 us
    dot_general x4, matrix products, level_step(): jnp.einsum('sbi,bio->sbo', field, cross_w, preferred_element_type=jnp.flo...  8.8 us
  transfers between devices with their start and end apart: 4, of which 4 were waited for; matrix products, arithmetic and copies ran while one was open for 1% of the time, Pallas kernels for 0%

commit v1 on v0

v1 whole, which is shorter than its diff:
```python
import functools

import jax
import jax.numpy as jnp
from jax import lax
from jax.experimental import pallas as pl
from jax.experimental.pallas import tpu as pltpu
from jax.sharding import PartitionSpec as P

MESH = pl.DeviceIdType.MESH
BF = jnp.bfloat16
F32 = jnp.float32
CHUNKS = 8
GROUP_ROWS = 256


def mm(a, b):
    return jnp.dot(a, b, preferred_element_type=F32)


def finish(v):
    return jnp.maximum(v, 0.0).astype(BF)


def quarters(tiles):
    return [
        jnp.concatenate([tile[:, 32 * j : 32 * j + 32] for tile in tiles], axis=1)
        for j in range(4)
    ]


def ring(v):
    return lax.rem(v + 8, 4)


def kernel(
    chunks, rows,
    x_hbm, sw_hbm, cw_hbm, lb, gw_hbm, gb, o_hbm,
    xio, xh, ts, tr, hb, h2, ab, mx, zb, h3, rb,
    w1s, w1c, w2s, w2c, ws, wzs, wzc, b2, bz, pin, pout,
    xin_sem, xout_sem, local_sem, w_send, w_recv,
    t_send, t_recv, h_send, h_recv, a_send, a_recv, z_send, z_recv, r_send, r_recv,
):
    s, t = lax.axis_index("src"), lax.axis_index("tgt")
    core, z, x_lo = lax.rem(s, 2), lax.rem(s // 2, 4), s // 8
    x_hi, y = lax.rem(t, 2), t // 2
    x = x_hi * 2 + x_lo

    def dev(x_, y_, z_, core_):
        return ((lax.rem(x_, 2) * 4 + z_) * 2 + core_, y_ * 2 + x_ // 2)

    core_peer = dev(x, y, z, 1 - core)
    x_peer = dev(x_hi * 2 + 1 - x_lo, y, z, core)

    def z_peer(k):
        return dev(x, y, ring(z + k), core)

    def xy_peer(w):
        return dev(ring(x + w // 4), ring(y + lax.rem(w, 4)), z, core)

    span = rows * 8

    def x_copy(c):
        part = pl.ds(pl.multiple_of(c * span, span), span)
        return pltpu.make_async_copy(x_hbm.at[part], xio.at[c], xin_sem.at[c])

    def o_copy(c):
        part = pl.ds(pl.multiple_of(c * span, span), span)
        return pltpu.make_async_copy(xio.at[c], o_hbm.at[part], xout_sem.at[c])

    local = [
        pltpu.make_async_copy(cw_hbm.at[0], w1c, local_sem.at[0]),
        pltpu.make_async_copy(sw_hbm.at[0], w1s, local_sem.at[1]),
        pltpu.make_async_copy(sw_hbm.at[1, pl.ds(4 * x_lo, 4)], w2s.at[pl.ds(0, 4)], local_sem.at[2]),
        pltpu.make_async_copy(cw_hbm.at[1, pl.ds(4 * x_lo, 4)], w2c.at[pl.ds(0, 4)], local_sem.at[3]),
        pltpu.make_async_copy(gw_hbm, ws, local_sem.at[4]),
        pltpu.make_async_copy(sw_hbm.at[pl.ds(2, 2), pl.ds(2 * z, 2)], wzs.at[0], local_sem.at[5]),
        pltpu.make_async_copy(cw_hbm.at[pl.ds(2, 2), pl.ds(2 * z, 2)], wzc.at[0], local_sem.at[6]),
    ]
    x_copy(0).start()
    for copy in local[:2]:
        copy.start()

    barrier = pltpu.get_barrier_semaphore()

    def greet(device):
        pl.semaphore_signal(barrier, inc=1, device_id=device, device_id_type=MESH)

    greet(core_peer)
    for w in range(1, 16):
        greet(xy_peer(w))
    for k in range(1, 4):
        greet(z_peer(k))

    row = lax.broadcasted_iota(jnp.int32, (GROUP_ROWS, GROUP_ROWS), 0)
    col = lax.broadcasted_iota(jnp.int32, (GROUP_ROWS, GROUP_ROWS), 1)
    pin[...] = jnp.where(col == lax.rem(row, 32) * 8 + row // 32, 1.0, 0.0).astype(BF)
    pout[...] = jnp.where(row == lax.rem(col, 32) * 8 + col // 32, 1.0, 0.0).astype(BF)
    bz[0] = lb[pl.ds(2, 2)]

    pl.semaphore_wait(barrier, 19)

    def send(src, dst, send_sem, recv_sem, device):
        pltpu.make_async_remote_copy(
            src_ref=src, dst_ref=dst, send_sem=send_sem, recv_sem=recv_sem,
            device_id=device, device_id_type=MESH,
        ).start()

    def settle(ref, sem):
        pltpu.make_async_copy(ref, ref, sem).wait()

    away = pl.ds(4 * (1 - x_lo), 4)
    send(sw_hbm.at[1, away], w2s.at[pl.ds(4, 4)], w_send.at[0], w_recv.at[0], x_peer)
    send(cw_hbm.at[1, away], w2c.at[pl.ds(4, 4)], w_send.at[1], w_recv.at[1], x_peer)
    send(lb.at[1], b2, w_send.at[2], w_recv.at[2], x_peer)
    for k in range(1, 4):
        blocks = pl.ds(2 * ring(z + k), 2)
        send(sw_hbm.at[pl.ds(2, 2), blocks], wzs.at[k], w_send.at[3], w_recv.at[3], z_peer(k))
        send(cw_hbm.at[pl.ds(2, 2), blocks], wzc.at[k], w_send.at[4], w_recv.at[4], z_peer(k))
        send(lb.at[pl.ds(2, 2)], bz.at[k], w_send.at[5], w_recv.at[5], z_peer(k))
    for copy in local[2:]:
        copy.start()

    @pl.loop(1, chunks)
    def _(c):
        x_copy(c).start()

    local[0].wait()

    def term_stage(c):
        x_copy(c).wait()

        @pl.loop(0, rows // 32)
        def _(g):
            part = pl.ds(pl.multiple_of(g * GROUP_ROWS, GROUP_ROWS), GROUP_ROWS)
            v = mm(pin[...], xio[c, part]).astype(BF)
            dst = pl.ds(pl.multiple_of(g * 32, 32), 32)
            for l in range(8):
                xh[c, l, dst] = v[32 * l : 32 * l + 32]

        @pl.loop(0, 8)
        def _(l):
            ts[c, l] = mm(xh[c, l], w1c[l]).astype(BF)

        send(ts.at[c], tr.at[c], t_send, t_recv.at[c], core_peer)

    def first_stage(c):
        settle(tr.at[c], t_recv.at[c])

        @pl.loop(0, 8)
        def _(l):
            v = mm(xh[c, l], w1s[l]) + tr[c, l].astype(F32) + lb[0, pl.ds(l, 1)]
            hb[c, l] = finish(v)

        send(hb.at[c, away], hb.at[c, pl.ds(8, 4)], h_send, h_recv.at[c], x_peer)

    def second_stage(c):
        settle(hb.at[c, pl.ds(8, 4)], h_recv.at[c])

        @pl.loop(0, 4)
        def _(m):
            l = 4 * x_lo + m
            mine, other = hb[c, l], hb[c, 8 + m]
            h2[m] = finish(mm(mine, w2s[m]) + mm(other, w2c[4 + m]) + lb[1, pl.ds(l, 1)])
            h2[4 + m] = finish(mm(other, w2s[4 + m]) + mm(mine, w2c[m]) + b2[pl.ds(l, 1)])

        @pl.loop(0, 2)
        def _(side):
            x_to = x_lo + side - 2 * x_lo * side
            for half in range(2):
                lanes = pl.ds(128 * half, 128)
                out = quarters([h2[4 * side + m, :, lanes] for m in range(4)])
                for u in range(4):
                    j = 4 * half + u
                    r = ring((j % 2) * 2 + x_to - x)
                    q = ring(j // 2 - y)
                    ab[c, r * 4 + q] = out[u]

        for w in range(1, 16):
            send(ab.at[c, w], ab.at[c, 15 + w], a_send, a_recv.at[c], xy_peer(w))

    def switch_stage(c):
        settle(ab.at[c, pl.ds(16, 15)], a_recv.at[c])

        @pl.loop(0, 2)
        def _(e):
            for half in range(2):
                tiles = []
                for u in range(4):
                    g = 4 * half + u
                    r = ring(x - ((g % 2) * 2 + e))
                    q = ring(y - g // 2)
                    w = r * 4 + q
                    tiles.append(ab[c, w + 15 * jnp.minimum(w, 1)])
                out = quarters(tiles)
                for m in range(4):
                    mx[4 * e + m, :, pl.ds(128 * half, 128)] = out[m]

        @pl.loop(0, 8)
        def _(l):
            v = mm(mx[l], ws[l]) + gb[pl.ds(l, 1)]
            zb[c, ring(l // 2 - z), lax.rem(l, 2)] = finish(v)

        for k in range(1, 4):
            send(zb.at[c, k], zb.at[c, 3 + k], z_send, z_recv.at[c], z_peer(k))

    def last_stage(c):
        settle(zb.at[c, pl.ds(4, 3)], z_recv.at[c])

        @pl.loop(0, 2)
        def _(n):
            bias = pl.ds(2 * z + n, 1)

            @pl.loop(0, 4)
            def _(k):
                k2 = lax.rem(k + 2, 4)
                a = zb[c, k + 3 * jnp.minimum(k, 1), n]
                b = zb[c, k2 + 3 * jnp.minimum(k2, 1), n]
                h3[k] = finish(mm(a, wzs[k, 0, n]) + mm(b, wzc[k2, 0, n]) + bz[k, 0, bias])

            @pl.loop(0, 4)
            def _(k):
                home = ring(z - k)
                k1 = ring(z - (home + 1 - 2 * lax.rem(home, 2)))
                v = mm(h3[k], wzs[k, 1, n]) + mm(h3[k1], wzc[k1, 1, n]) + bz[k, 1, bias]
                rb[c, k, n] = finish(v)

        for k in range(1, 4):
            send(rb.at[c, k], rb.at[c, 3 + k], r_send, r_recv.at[c], z_peer(4 - k))

    def output_stage(c):
        settle(rb.at[c, pl.ds(4, 3)], r_recv.at[c])

        @pl.loop(0, rows // 32)
        def _(g):
            src = pl.ds(pl.multiple_of(g * 32, 32), 32)
            parts = []
            for l in range(8):
                k = ring(l // 2 - z)
                parts.append(rb[c, k + 3 * jnp.minimum(k, 1), l % 2, src])
            v = mm(pout[...], jnp.concatenate(parts, axis=0)).astype(BF)
            xio[c, pl.ds(pl.multiple_of(g * GROUP_ROWS, GROUP_ROWS), GROUP_ROWS)] = v

        o_copy(c).start()

    term_stage(0)
    local[1].wait()

    @pl.loop(0, chunks + 4)
    def _(step):
        @pl.when(step + 1 < chunks)
        def _():
            term_stage(step + 1)

        @pl.when(step < chunks)
        def _():
            first_stage(step)

        @pl.when(step == 1)
        def _():
            for copy in local[2:5]:
                copy.wait()
            settle(w2s.at[pl.ds(4, 4)], w_recv.at[0])
            settle(w2c.at[pl.ds(4, 4)], w_recv.at[1])
            settle(b2, w_recv.at[2])

        @pl.when((step >= 1) & (step <= chunks))
        def _():
            second_stage(step - 1)

        @pl.when((step >= 2) & (step <= chunks + 1))
        def _():
            switch_stage(step - 2)

        @pl.when(step == 3)
        def _():
            for copy in local[5:]:
                copy.wait()
            settle(wzs.at[pl.ds(1, 3)], w_recv.at[3])
            settle(wzc.at[pl.ds(1, 3)], w_recv.at[4])
            settle(bz.at[pl.ds(1, 3)], w_recv.at[5])

        @pl.when((step >= 3) & (step <= chunks + 2))
        def _():
            last_stage(step - 3)

        @pl.when(step >= 4)
        def _():
            output_stage(step - 4)

    settle(w2s.at[pl.ds(4, 4)], w_send.at[0])
    settle(w2c.at[pl.ds(4, 4)], w_send.at[1])
    settle(b2, w_send.at[2])
    settle(wzs.at[pl.ds(1, 3)], w_send.at[3])
    settle(wzc.at[pl.ds(1, 3)], w_send.at[4])
    settle(bz.at[pl.ds(1, 3)], w_send.at[5])

    @pl.loop(0, chunks)
    def _(c):
        settle(ts.at[c], t_send)
        settle(hb.at[c, pl.ds(8, 4)], h_send)
        settle(ab.at[c, pl.ds(16, 15)], a_send)
        settle(zb.at[c, pl.ds(4, 3)], z_send)
        settle(rb.at[c, pl.ds(4, 3)], r_send)
        o_copy(c).wait()


def per_device(source_field, self_weight, cross_weight, level_bias, switch_weight, switch_bias):
    shots, blocks, width = source_field.shape
    chunks = CHUNKS
    rows = shots // chunks
    anywhere = pl.BlockSpec(memory_space=pl.ANY)
    vmem = pl.BlockSpec(memory_space=pltpu.VMEM)
    dma = pltpu.SemaphoreType.DMA
    square = (width, width)
    out = pl.pallas_call(
        functools.partial(kernel, chunks, rows),
        out_shape=jax.ShapeDtypeStruct((shots * blocks, width), BF),
        in_specs=[anywhere, anywhere, anywhere, vmem, anywhere, vmem],
        out_specs=anywhere,
        scratch_shapes=[
            pltpu.VMEM((chunks, rows * 8, width), BF),
            pltpu.VMEM((chunks, 8, rows, width), BF),
            pltpu.VMEM((chunks, 8, rows, width), BF),
            pltpu.VMEM((chunks, 8, rows, width), BF),
            pltpu.VMEM((chunks, 12, rows, width), BF),
            pltpu.VMEM((8, rows, width), BF),
            pltpu.VMEM((chunks, 31, rows, 128), BF),
            pltpu.VMEM((8, rows, width), BF),
            pltpu.VMEM((chunks, 7, 2, rows, width), BF),
            pltpu.VMEM((4, rows, width), BF),
            pltpu.VMEM((chunks, 7, 2, rows, width), BF),
            pltpu.VMEM((8,) + square, BF),
            pltpu.VMEM((8,) + square, BF),
            pltpu.VMEM((8,) + square, BF),
            pltpu.VMEM((8,) + square, BF),
            pltpu.VMEM((8,) + square, BF),
            pltpu.VMEM((4, 2, 2) + square, BF),
            pltpu.VMEM((4, 2, 2) + square, BF),
            pltpu.VMEM((8, width), F32),
            pltpu.VMEM((4, 2, 8, width), F32),
            pltpu.VMEM((GROUP_ROWS, GROUP_ROWS), BF),
            pltpu.VMEM((GROUP_ROWS, GROUP_ROWS), BF),
            dma((chunks,)), dma((chunks,)), dma((7,)), dma((6,)), dma((6,)),
            dma, dma((chunks,)),
            dma, dma((chunks,)),
            dma, dma((chunks,)),
            dma, dma((chunks,)),
            dma, dma((chunks,)),
        ],
        compiler_params=pltpu.CompilerParams(
            collective_id=0, has_side_effects=True, vmem_limit_bytes=64 * 1024 * 1024 - 65536
        ),
        name="butterfly",
    )(
        source_field.reshape(shots * blocks, width),
        self_weight, cross_weight, level_bias, switch_weight, switch_bias,
    )
    return out.reshape(shots, blocks, width)


def solution(mesh):
    placed = (
        P(None, ("src", "tgt"), None),
        P(None, ("src", "tgt"), None, None),
        P(None, ("src", "tgt"), None, None),
        P(None, ("src", "tgt"), None),
        P(("src", "tgt"), None, None),
        P(("src", "tgt"), None),
    )
    return jax.shard_map(
        per_device,
        mesh=mesh,
        in_specs=placed,
        out_specs=P(None, ("src", "tgt"), None),
        check_vma=False,
    )
```

time: 376 us -> 159 us (0.42)
  waiting for transfers between devices: 270 us -> 0 us
  Pallas kernels: 0 us -> 153 us
  blocking collectives: 57.2 us -> 0 us
  matrix products: 28.3 us -> 0 us
  starting transfers between devices: 7.12 us -> 0 us
  local copies, waits for them, and re-layouts: 10.1 us -> 4.47 us
    ppermute x4 -> x0, waiting for transfers between devices: 270 us -> none  [from_partner(): lax.ppermute(value, axis, [(i, i ^ 1 << apart) for i in range(lax.axis_si...]
    pallas_call x0 -> x1, Pallas kernels: none -> 153 us  [per_device(): pl.pallas_call(functools.partial(kernel, chunks, rows), out_shape=jax.Sha...]
    all_to_all x1 -> x0, blocking collectives: 57.2 us -> none  [per_device(): lax.all_to_all(field, 'tgt', split_axis=2, concat_axis=2, tiled=True)]
    dot_general x9 -> x0, matrix products: 28.3 us -> none  [the longest x4 14.2 us: level_step(): jnp.einsum('sbi,bio->sbo', field, self_w, preferred_element_type=jnp.floa...]
    convert_element_type x2 -> x0, local copies, waits for them, and re-layouts: 9.19 us -> none  [level_step(): jax.nn.relu(own_part + term.astype(jnp.float32) + bias[None])]
    ppermute x4 -> x0, starting transfers between devices: 7.12 us -> none  [from_partner(): lax.ppermute(value, axis, [(i, i ^ 1 << apart) for i in range(lax.axis_si...]
  transfers between devices with their start and end apart: 4 -> 0, of which waited for: 4 -> 0; matrix products, arithmetic and copies ran while one was open for 1% -> 0% of each run, Pallas kernels for 0% -> 0%
where the time goes in v1:
time: 159 us; the launch traced here: 158 us
  Pallas kernels  153 us (96%)
  local copies, waits for them, and re-layouts  4.47 us (3%)
    pallas_call x1, Pallas kernels, per_device(): pl.pallas_call(functools.partial(kernel, chunks, rows), out_shape=jax.Sha...  153 us
    unnamed x1, local copies, waits for them, and re-layouts  4.47 us

profile of v1, /device:TPU:0, one launch (start us, length us, event | category | flops | bytes accessed | tf_op | source)
XLA Modules:
  0.0 157.6 jit_solution(15964677451142754406)
XLA Ops:
  0.0 153.1 %butterfly.1 = bf16[8192,256]{1,0:T(8,128)(2,1)} custom-call(bf16[8192,256]{1,0:T(8,128)(2,1)} %bitcast.3, bf16[4,8,256,256]{3,2,1,0:T(8,128)(2,1)} %sw_hbm.1, bf16[4,8,256,256]{3,2,1,0:T(8,128)(2,1)} %cw_hbm.1, f32[4,8,256]{2,1,0:T(8,128)} %lb.1, bf16[8,256,256]{2,1,0:T(8,128)(2,1)} %gw_hbm.1, f32[8,256]{1,0:T(8,128)} %gb.1), custom_call_target="tpu_custom_call" | custom-call | tf_op jit(solution)/shard_map/butterfly/pallas_call | solution.py:316
  153.1 4.5 %copy.8 = bf16[1024,8,256]{2,1,0:T(8,128)(2,1)} copy(bf16[1024,8,256]{2,1,0:T(8,128)(2,1)} %bitcast.2) | data formatting | bytes 8388608

commit v2 on v1

--- a/solution.py
+++ b/solution.py
@@ -130,16 +130,14 @@
     def term_stage(c):
         x_copy(c).wait()
 
-        @pl.loop(0, rows // 32)
-        def _(g):
+        for g in range(rows // 32):
             part = pl.ds(pl.multiple_of(g * GROUP_ROWS, GROUP_ROWS), GROUP_ROWS)
             v = mm(pin[...], xio[c, part]).astype(BF)
             dst = pl.ds(pl.multiple_of(g * 32, 32), 32)
             for l in range(8):
                 xh[c, l, dst] = v[32 * l : 32 * l + 32]
 
-        @pl.loop(0, 8)
-        def _(l):
+        for l in range(8):
             ts[c, l] = mm(xh[c, l], w1c[l]).astype(BF)
 
         send(ts.at[c], tr.at[c], t_send, t_recv.at[c], core_peer)
@@ -147,8 +145,7 @@
     def first_stage(c):
         settle(tr.at[c], t_recv.at[c])
 
-        @pl.loop(0, 8)
-        def _(l):
+        for l in range(8):
             v = mm(xh[c, l], w1s[l]) + tr[c, l].astype(F32) + lb[0, pl.ds(l, 1)]
             hb[c, l] = finish(v)
 
@@ -157,15 +154,13 @@
     def second_stage(c):
         settle(hb.at[c, pl.ds(8, 4)], h_recv.at[c])
 
-        @pl.loop(0, 4)
-        def _(m):
+        for m in range(4):
             l = 4 * x_lo + m
             mine, other = hb[c, l], hb[c, 8 + m]
             h2[m] = finish(mm(mine, w2s[m]) + mm(other, w2c[4 + m]) + lb[1, pl.ds(l, 1)])
             h2[4 + m] = finish(mm(other, w2s[4 + m]) + mm(mine, w2c[m]) + b2[pl.ds(l, 1)])
 
-        @pl.loop(0, 2)
-        def _(side):
+        for side in range(2):
             x_to = x_lo + side - 2 * x_lo * side
             for half in range(2):
                 lanes = pl.ds(128 * half, 128)
@@ -182,8 +177,7 @@
     def switch_stage(c):
         settle(ab.at[c, pl.ds(16, 15)], a_recv.at[c])
 
-        @pl.loop(0, 2)
-        def _(e):
+        for e in range(2):
             for half in range(2):
                 tiles = []
                 for u in range(4):
@@ -196,8 +190,7 @@
                 for m in range(4):
                     mx[4 * e + m, :, pl.ds(128 * half, 128)] = out[m]
 
-        @pl.loop(0, 8)
-        def _(l):
+        for l in range(8):
             v = mm(mx[l], ws[l]) + gb[pl.ds(l, 1)]
             zb[c, ring(l // 2 - z), lax.rem(l, 2)] = finish(v)
 
@@ -207,19 +200,16 @@
     def last_stage(c):
         settle(zb.at[c, pl.ds(4, 3)], z_recv.at[c])
 
-        @pl.loop(0, 2)
-        def _(n):
+        for n in range(2):
             bias = pl.ds(2 * z + n, 1)
 
-            @pl.loop(0, 4)
-            def _(k):
+            for k in range(4):
                 k2 = lax.rem(k + 2, 4)
                 a = zb[c, k + 3 * jnp.minimum(k, 1), n]
                 b = zb[c, k2 + 3 * jnp.minimum(k2, 1), n]
                 h3[k] = finish(mm(a, wzs[k, 0, n]) + mm(b, wzc[k2, 0, n]) + bz[k, 0, bias])
 
-            @pl.loop(0, 4)
-            def _(k):
+            for k in range(4):
                 home = ring(z - k)
                 k1 = ring(z - (home + 1 - 2 * lax.rem(home, 2)))
                 v = mm(h3[k], wzs[k, 1, n]) + mm(h3[k1], wzc[k1, 1, n]) + bz[k, 1, bias]
@@ -231,8 +221,7 @@
     def output_stage(c):
         settle(rb.at[c, pl.ds(4, 3)], r_recv.at[c])
 
-        @pl.loop(0, rows // 32)
-        def _(g):
+        for g in range(rows // 32):
             src = pl.ds(pl.multiple_of(g * 32, 32), 32)
             parts = []
             for l in range(8):

time: 159 us -> 154 us (0.969)
  Pallas kernels: 153 us -> 150 us
    pallas_call x1, Pallas kernels: 153 us -> 150 us  [per_device(): pl.pallas_call(functools.partial(kernel, chunks, rows), out_shape=jax.Sha...]
where the time goes in v2:
time: 154 us
  Pallas kernels  150 us (97%)
  local copies, waits for them, and re-layouts  4.47 us (3%)
    pallas_call x1, Pallas kernels, per_device(): pl.pallas_call(functools.partial(kernel, chunks, rows), out_shape=jax.Sha...  150 us
    unnamed x1, local copies, waits for them, and re-layouts  4.47 us

profile of v2, /device:TPU:0, one launch (start us, length us, event | category | flops | bytes accessed | tf_op | source)
XLA Modules:
  0.0 154.1 jit_solution(10888100936545285860)
XLA Ops:
  0.0 149.6 %butterfly.1 = bf16[8192,256]{1,0:T(8,128)(2,1)} custom-call(bf16[8192,256]{1,0:T(8,128)(2,1)} %bitcast.3, bf16[4,8,256,256]{3,2,1,0:T(8,128)(2,1)} %sw_hbm.1, bf16[4,8,256,256]{3,2,1,0:T(8,128)(2,1)} %cw_hbm.1, f32[4,8,256]{2,1,0:T(8,128)} %lb.1, bf16[8,256,256]{2,1,0:T(8,128)(2,1)} %gw_hbm.1, f32[8,256]{1,0:T(8,128)} %gb.1), custom_call_target="tpu_custom_call" | custom-call | tf_op jit(solution)/shard_map/butterfly/pallas_call | solution.py:305
  149.6 4.5 %copy.8 = bf16[1024,8,256]{2,1,0:T(8,128)(2,1)} copy(bf16[1024,8,256]{2,1,0:T(8,128)(2,1)} %bitcast.2) | data formatting | bytes 8388608

commit v3 on v2

--- a/solution.py
+++ b/solution.py
@@ -35,10 +35,10 @@
 
 def kernel(
     chunks, rows,
-    x_hbm, sw_hbm, cw_hbm, lb, gw_hbm, gb, o_hbm,
+    x_hbm, sw_hbm, cw_hbm, lb_hbm, gw_hbm, gb_hbm, out_ref,
     xio, xh, ts, tr, hb, h2, ab, mx, zb, h3, rb,
-    w1s, w1c, w2s, w2c, ws, wzs, wzc, b2, bz, pin, pout,
-    xin_sem, xout_sem, local_sem, w_send, w_recv,
+    w1s, w1c, w2s, w2c, ws, wzs, wzc, lb, gb, b2, bz, pin, pout,
+    xin_sem, local_sem, w_send, w_recv,
     t_send, t_recv, h_send, h_recv, a_send, a_recv, z_send, z_recv, r_send, r_recv,
 ):
     s, t = lax.axis_index("src"), lax.axis_index("tgt")
@@ -64,21 +64,20 @@
         part = pl.ds(pl.multiple_of(c * span, span), span)
         return pltpu.make_async_copy(x_hbm.at[part], xio.at[c], xin_sem.at[c])
 
-    def o_copy(c):
-        part = pl.ds(pl.multiple_of(c * span, span), span)
-        return pltpu.make_async_copy(xio.at[c], o_hbm.at[part], xout_sem.at[c])
-
     local = [
         pltpu.make_async_copy(cw_hbm.at[0], w1c, local_sem.at[0]),
         pltpu.make_async_copy(sw_hbm.at[0], w1s, local_sem.at[1]),
+        pltpu.make_async_copy(lb_hbm, lb, local_sem.at[7]),
         pltpu.make_async_copy(sw_hbm.at[1, pl.ds(4 * x_lo, 4)], w2s.at[pl.ds(0, 4)], local_sem.at[2]),
         pltpu.make_async_copy(cw_hbm.at[1, pl.ds(4 * x_lo, 4)], w2c.at[pl.ds(0, 4)], local_sem.at[3]),
         pltpu.make_async_copy(gw_hbm, ws, local_sem.at[4]),
+        pltpu.make_async_copy(gb_hbm, gb, local_sem.at[8]),
         pltpu.make_async_copy(sw_hbm.at[pl.ds(2, 2), pl.ds(2 * z, 2)], wzs.at[0], local_sem.at[5]),
         pltpu.make_async_copy(cw_hbm.at[pl.ds(2, 2), pl.ds(2 * z, 2)], wzc.at[0], local_sem.at[6]),
+        pltpu.make_async_copy(lb_hbm.at[pl.ds(2, 2)], bz.at[0], local_sem.at[9]),
     ]
     x_copy(0).start()
-    for copy in local[:2]:
+    for copy in local[:3]:
         copy.start()
 
     barrier = pltpu.get_barrier_semaphore()
@@ -96,7 +95,6 @@
     col = lax.broadcasted_iota(jnp.int32, (GROUP_ROWS, GROUP_ROWS), 1)
     pin[...] = jnp.where(col == lax.rem(row, 32) * 8 + row // 32, 1.0, 0.0).astype(BF)
     pout[...] = jnp.where(row == lax.rem(col, 32) * 8 + col // 32, 1.0, 0.0).astype(BF)
-    bz[0] = lb[pl.ds(2, 2)]
 
     pl.semaphore_wait(barrier, 19)
 
@@ -112,13 +110,13 @@
     away = pl.ds(4 * (1 - x_lo), 4)
     send(sw_hbm.at[1, away], w2s.at[pl.ds(4, 4)], w_send.at[0], w_recv.at[0], x_peer)
     send(cw_hbm.at[1, away], w2c.at[pl.ds(4, 4)], w_send.at[1], w_recv.at[1], x_peer)
-    send(lb.at[1], b2, w_send.at[2], w_recv.at[2], x_peer)
-    for k in range(1, 4):
+    send(lb_hbm.at[1], b2, w_send.at[2], w_recv.at[2], x_peer)
+    for k in (1, 3, 2):
         blocks = pl.ds(2 * ring(z + k), 2)
         send(sw_hbm.at[pl.ds(2, 2), blocks], wzs.at[k], w_send.at[3], w_recv.at[3], z_peer(k))
         send(cw_hbm.at[pl.ds(2, 2), blocks], wzc.at[k], w_send.at[4], w_recv.at[4], z_peer(k))
-        send(lb.at[pl.ds(2, 2)], bz.at[k], w_send.at[5], w_recv.at[5], z_peer(k))
-    for copy in local[2:]:
+        send(lb_hbm.at[pl.ds(2, 2)], bz.at[k], w_send.at[5], w_recv.at[5], z_peer(k))
+    for copy in local[3:]:
         copy.start()
 
     @pl.loop(1, chunks)
@@ -144,12 +142,13 @@
 
     def first_stage(c):
         settle(tr.at[c], t_recv.at[c])
-
-        for l in range(8):
-            v = mm(xh[c, l], w1s[l]) + tr[c, l].astype(F32) + lb[0, pl.ds(l, 1)]
-            hb[c, l] = finish(v)
-
-        send(hb.at[c, away], hb.at[c, pl.ds(8, 4)], h_send, h_recv.at[c], x_peer)
+        for side in range(2):
+            for m in range(4):
+                l = 4 * (1 - x_lo if side == 0 else x_lo) + m
+                v = mm(xh[c, l], w1s[l]) + tr[c, l].astype(F32) + lb[0, pl.ds(l, 1)]
+                hb[c, l] = finish(v)
+            if side == 0:
+                send(hb.at[c, away], hb.at[c, pl.ds(8, 4)], h_send, h_recv.at[c], x_peer)
 
     def second_stage(c):
         settle(hb.at[c, pl.ds(8, 4)], h_recv.at[c])
@@ -170,7 +169,6 @@
                     r = ring((j % 2) * 2 + x_to - x)
                     q = ring(j // 2 - y)
                     ab[c, r * 4 + q] = out[u]
-
         for w in range(1, 16):
             send(ab.at[c, w], ab.at[c, 15 + w], a_send, a_recv.at[c], xy_peer(w))
 
@@ -190,50 +188,45 @@
                 for m in range(4):
                     mx[4 * e + m, :, pl.ds(128 * half, 128)] = out[m]
 
-        for l in range(8):
-            v = mm(mx[l], ws[l]) + gb[pl.ds(l, 1)]
-            zb[c, ring(l // 2 - z), lax.rem(l, 2)] = finish(v)
-
-        for k in range(1, 4):
-            send(zb.at[c, k], zb.at[c, 3 + k], z_send, z_recv.at[c], z_peer(k))
+        for n in range(2):
+            for k in (1, 3, 2, 0):
+                l = 2 * ring(z + k) + n
+                zb[c, n, k] = finish(mm(mx[l], ws[l]) + gb[pl.ds(l, 1)])
+            for k in (1, 3, 2):
+                send(zb.at[c, n, k], zb.at[c, n, 3 + k], z_send, z_recv.at[c, n], z_peer(k))
 
     def last_stage(c):
-        settle(zb.at[c, pl.ds(4, 3)], z_recv.at[c])
-
         for n in range(2):
+            settle(zb.at[c, n, pl.ds(4, 3)], z_recv.at[c, n])
             bias = pl.ds(2 * z + n, 1)
-
+            held = [zb[c, n, k + 3 if k else 0] for k in range(4)]
             for k in range(4):
-                k2 = lax.rem(k + 2, 4)
-                a = zb[c, k + 3 * jnp.minimum(k, 1), n]
-                b = zb[c, k2 + 3 * jnp.minimum(k2, 1), n]
-                h3[k] = finish(mm(a, wzs[k, 0, n]) + mm(b, wzc[k2, 0, n]) + bz[k, 0, bias])
-
-            for k in range(4):
+                k2 = (k + 2) % 4
+                v = mm(held[k], wzs[k, 0, n]) + mm(held[k2], wzc[k2, 0, n]) + bz[k, 0, bias]
+                h3[n, k] = finish(v)
+            for k in (1, 3, 2, 0):
                 home = ring(z - k)
                 k1 = ring(z - (home + 1 - 2 * lax.rem(home, 2)))
-                v = mm(h3[k], wzs[k, 1, n]) + mm(h3[k1], wzc[k1, 1, n]) + bz[k, 1, bias]
-                rb[c, k, n] = finish(v)
-
-        for k in range(1, 4):
-            send(rb.at[c, k], rb.at[c, 3 + k], r_send, r_recv.at[c], z_peer(4 - k))
+                v = mm(h3[n, k], wzs[k, 1, n]) + mm(h3[n, k1], wzc[k1, 1, n]) + bz[k, 1, bias]
+                rb[c, n, k] = finish(v)
+            for k in (1, 3, 2):
+                send(rb.at[c, n, k], rb.at[c, n, 3 + k], r_send, r_recv.at[c], z_peer(4 - k))
 
     def output_stage(c):
-        settle(rb.at[c, pl.ds(4, 3)], r_recv.at[c])
+        settle(rb.at[c, :, pl.ds(4, 3)], r_recv.at[c])
 
         for g in range(rows // 32):
             src = pl.ds(pl.multiple_of(g * 32, 32), 32)
             parts = []
             for l in range(8):
                 k = ring(l // 2 - z)
-                parts.append(rb[c, k + 3 * jnp.minimum(k, 1), l % 2, src])
+                parts.append(rb[c, l % 2, k + 3 * jnp.minimum(k, 1), src])
             v = mm(pout[...], jnp.concatenate(parts, axis=0)).astype(BF)
-            xio[c, pl.ds(pl.multiple_of(g * GROUP_ROWS, GROUP_ROWS), GROUP_ROWS)] = v
-
-        o_copy(c).start()
+            out_ref[pl.ds(pl.multiple_of(c * span + g * GROUP_ROWS, GROUP_ROWS), GROUP_ROWS)] = v
 
     term_stage(0)
-    local[1].wait()
+    for copy in local[1:3]:
+        copy.wait()
 
     @pl.loop(0, chunks + 4)
     def _(step):
@@ -247,7 +240,7 @@
 
         @pl.when(step == 1)
         def _():
-            for copy in local[2:5]:
+            for copy in local[3:7]:
                 copy.wait()
             settle(w2s.at[pl.ds(4, 4)], w_recv.at[0])
             settle(w2c.at[pl.ds(4, 4)], w_recv.at[1])
@@ -263,7 +256,7 @@
 
         @pl.when(step == 3)
         def _():
-            for copy in local[5:]:
+            for copy in local[7:]:
                 copy.wait()
             settle(wzs.at[pl.ds(1, 3)], w_recv.at[3])
             settle(wzc.at[pl.ds(1, 3)], w_recv.at[4])
@@ -289,9 +282,8 @@
         settle(ts.at[c], t_send)
         settle(hb.at[c, pl.ds(8, 4)], h_send)
         settle(ab.at[c, pl.ds(16, 15)], a_send)
-        settle(zb.at[c, pl.ds(4, 3)], z_send)
-        settle(rb.at[c, pl.ds(4, 3)], r_send)
-        o_copy(c).wait()
+        settle(zb.at[c, :, pl.ds(4, 3)], z_send)
+        settle(rb.at[c, :, pl.ds(4, 3)], r_send)
 
 
 def per_device(source_field, self_weight, cross_weight, level_bias, switch_weight, switch_bias):
@@ -304,9 +296,9 @@
     square = (width, width)
     out = pl.pallas_call(
         functools.partial(kernel, chunks, rows),
-        out_shape=jax.ShapeDtypeStruct((shots * blocks, width), BF),
-        in_specs=[anywhere, anywhere, anywhere, vmem, anywhere, vmem],
-        out_specs=anywhere,
+        out_shape=pltpu.VMEM((shots * blocks, width), BF),
+        in_specs=[anywhere] * 6,
+        out_specs=vmem,
         scratch_shapes=[
             pltpu.VMEM((chunks, rows * 8, width), BF),
             pltpu.VMEM((chunks, 8, rows, width), BF),
@@ -316,9 +308,9 @@
             pltpu.VMEM((8, rows, width), BF),
             pltpu.VMEM((chunks, 31, rows, 128), BF),
             pltpu.VMEM((8, rows, width), BF),
-            pltpu.VMEM((chunks, 7, 2, rows, width), BF),
-            pltpu.VMEM((4, rows, width), BF),
-            pltpu.VMEM((chunks, 7, 2, rows, width), BF),
+            pltpu.VMEM((chunks, 2, 7, rows, width), BF),
+            pltpu.VMEM((2, 4, rows, width), BF),
+            pltpu.VMEM((chunks, 2, 7, rows, width), BF),
             pltpu.VMEM((8,) + square, BF),
             pltpu.VMEM((8,) + square, BF),
             pltpu.VMEM((8,) + square, BF),
@@ -326,19 +318,21 @@
             pltpu.VMEM((8,) + square, BF),
             pltpu.VMEM((4, 2, 2) + square, BF),
             pltpu.VMEM((4, 2, 2) + square, BF),
+            pltpu.VMEM((4, 8, width), F32),
+            pltpu.VMEM((8, width), F32),
             pltpu.VMEM((8, width), F32),
             pltpu.VMEM((4, 2, 8, width), F32),
             pltpu.VMEM((GROUP_ROWS, GROUP_ROWS), BF),
             pltpu.VMEM((GROUP_ROWS, GROUP_ROWS), BF),
-            dma((chunks,)), dma((chunks,)), dma((7,)), dma((6,)), dma((6,)),
+            dma((chunks,)), dma((10,)), dma((6,)), dma((6,)),
             dma, dma((chunks,)),
             dma, dma((chunks,)),
             dma, dma((chunks,)),
-            dma, dma((chunks,)),
+            dma, dma((chunks, 2)),
             dma, dma((chunks,)),
         ],
         compiler_params=pltpu.CompilerParams(
-            collective_id=0, has_side_effects=True, vmem_limit_bytes=64 * 1024 * 1024 - 65536
+            collective_id=0, has_side_effects=True, vmem_limit_bytes=56 * 1024 * 1024
         ),
         name="butterfly",
     )(

time: 154 us -> 150 us (0.974)
  local copies, waits for them, and re-layouts: 4.47 us -> 2.02 us
  Pallas kernels: 150 us -> 148 us
    unnamed x1, local copies, waits for them, and re-layouts: 4.47 us -> 2.02 us
where the time goes in v3:
time: 150 us
  Pallas kernels  148 us (99%)
  local copies, waits for them, and re-layouts  2.02 us (1%)
    pallas_call x1, Pallas kernels, per_device(): pl.pallas_call(functools.partial(kernel, chunks, rows), out_shape=pltpu.V...  148 us

profile of v3, /device:TPU:0, one launch (start us, length us, event | category | flops | bytes accessed | tf_op | source)
XLA Modules:
  0.0 150.1 jit_solution(18072339235701900231)
XLA Ops:
  0.0 148.1 %butterfly.1 = bf16[8192,256]{1,0:T(8,128)(2,1)S(1)} custom-call(bf16[8192,256]{1,0:T(8,128)(2,1)} %bitcast.3, bf16[4,8,256,256]{3,2,1,0:T(8,128)(2,1)} %sw_hbm.1, bf16[4,8,256,256]{3,2,1,0:T(8,128)(2,1)} %cw_hbm.1, f32[4,8,256]{2,1,0:T(8,128)} %lb_hbm.1, bf16[8,256,256]{2,1,0:T(8,128)(2,1)} %gw_hbm.1, f32[8,256]{1,0:T(8,128)} %gb_hbm.1), custom_call_target="tpu_custom_call" | custom-call | tf_op jit(solution)/shard_map/butterfly/pallas_call | solution.py:297
  148.1 2.0 %copy.8 = bf16[1024,8,256]{2,1,0:T(8,128)(2,1)} copy(bf16[1024,8,256]{2,1,0:T(8,128)(2,1)S(1)} %bitcast.2) | data formatting | bytes 8388608

commit v4 on v3

--- a/solution.py
+++ b/solution.py
@@ -76,10 +76,6 @@
         pltpu.make_async_copy(cw_hbm.at[pl.ds(2, 2), pl.ds(2 * z, 2)], wzc.at[0], local_sem.at[6]),
         pltpu.make_async_copy(lb_hbm.at[pl.ds(2, 2)], bz.at[0], local_sem.at[9]),
     ]
-    x_copy(0).start()
-    for copy in local[:3]:
-        copy.start()
-
     barrier = pltpu.get_barrier_semaphore()
 
     def greet(device):
@@ -91,10 +87,9 @@
     for k in range(1, 4):
         greet(z_peer(k))
 
-    row = lax.broadcasted_iota(jnp.int32, (GROUP_ROWS, GROUP_ROWS), 0)
-    col = lax.broadcasted_iota(jnp.int32, (GROUP_ROWS, GROUP_ROWS), 1)
-    pin[...] = jnp.where(col == lax.rem(row, 32) * 8 + row // 32, 1.0, 0.0).astype(BF)
-    pout[...] = jnp.where(row == lax.rem(col, 32) * 8 + col // 32, 1.0, 0.0).astype(BF)
+    x_copy(0).start()
+    for copy in local[:3]:
+        copy.start()
 
     pl.semaphore_wait(barrier, 19)
 
@@ -122,6 +117,11 @@
     @pl.loop(1, chunks)
     def _(c):
         x_copy(c).start()
+
+    row = lax.broadcasted_iota(jnp.int32, (GROUP_ROWS, GROUP_ROWS), 0)
+    col = lax.broadcasted_iota(jnp.int32, (GROUP_ROWS, GROUP_ROWS), 1)
+    pin[...] = jnp.where(col == lax.rem(row, 32) * 8 + row // 32, 1.0, 0.0).astype(BF)
+    pout[...] = jnp.where(row == lax.rem(col, 32) * 8 + col // 32, 1.0, 0.0).astype(BF)
 
     local[0].wait()
 

time: 150 us -> 150 us (level)
  no operation moved by 1% of the time
where the time goes in v4:
time: 150 us
  Pallas kernels  148 us (99%)
  local copies, waits for them, and re-layouts  2.02 us (1%)
    pallas_call x1, Pallas kernels, per_device(): pl.pallas_call(functools.partial(kernel, chunks, rows), out_shape=pltpu.V...  148 us

profile of v4, /device:TPU:0, one launch (start us, length us, event | category | flops | bytes accessed | tf_op | source)
XLA Modules:
  0.0 150.1 jit_solution(15602224560738548101)
XLA Ops:
  0.0 148.0 %butterfly.1 = bf16[8192,256]{1,0:T(8,128)(2,1)S(1)} custom-call(bf16[8192,256]{1,0:T(8,128)(2,1)} %bitcast.3, bf16[4,8,256,256]{3,2,1,0:T(8,128)(2,1)} %sw_hbm.1, bf16[4,8,256,256]{3,2,1,0:T(8,128)(2,1)} %cw_hbm.1, f32[4,8,256]{2,1,0:T(8,128)} %lb_hbm.1, bf16[8,256,256]{2,1,0:T(8,128)(2,1)} %gw_hbm.1, f32[8,256]{1,0:T(8,128)} %gb_hbm.1), custom_call_target="tpu_custom_call" | custom-call | tf_op jit(solution)/shard_map/butterfly/pallas_call | solution.py:297
  148.0 2.0 %copy.8 = bf16[1024,8,256]{2,1,0:T(8,128)(2,1)} copy(bf16[1024,8,256]{2,1,0:T(8,128)(2,1)S(1)} %bitcast.2) | data formatting | bytes 8388608

commit v5 on v3

--- a/solution.py
+++ b/solution.py
@@ -111,7 +111,7 @@
     send(sw_hbm.at[1, away], w2s.at[pl.ds(4, 4)], w_send.at[0], w_recv.at[0], x_peer)
     send(cw_hbm.at[1, away], w2c.at[pl.ds(4, 4)], w_send.at[1], w_recv.at[1], x_peer)
     send(lb_hbm.at[1], b2, w_send.at[2], w_recv.at[2], x_peer)
-    for k in (1, 3, 2):
+    for k in (2, 1, 3):
         blocks = pl.ds(2 * ring(z + k), 2)
         send(sw_hbm.at[pl.ds(2, 2), blocks], wzs.at[k], w_send.at[3], w_recv.at[3], z_peer(k))
         send(cw_hbm.at[pl.ds(2, 2), blocks], wzc.at[k], w_send.at[4], w_recv.at[4], z_peer(k))
@@ -189,10 +189,10 @@
                     mx[4 * e + m, :, pl.ds(128 * half, 128)] = out[m]
 
         for n in range(2):
-            for k in (1, 3, 2, 0):
+            for k in (2, 1, 3, 0):
                 l = 2 * ring(z + k) + n
                 zb[c, n, k] = finish(mm(mx[l], ws[l]) + gb[pl.ds(l, 1)])
-            for k in (1, 3, 2):
+            for k in (2, 1, 3):
                 send(zb.at[c, n, k], zb.at[c, n, 3 + k], z_send, z_recv.at[c, n], z_peer(k))
 
     def last_stage(c):
@@ -204,12 +204,12 @@
                 k2 = (k + 2) % 4
                 v = mm(held[k], wzs[k, 0, n]) + mm(held[k2], wzc[k2, 0, n]) + bz[k, 0, bias]
                 h3[n, k] = finish(v)
-            for k in (1, 3, 2, 0):
+            for k in (2, 1, 3, 0):
                 home = ring(z - k)
                 k1 = ring(z - (home + 1 - 2 * lax.rem(home, 2)))
                 v = mm(h3[n, k], wzs[k, 1, n]) + mm(h3[n, k1], wzc[k1, 1, n]) + bz[k, 1, bias]
                 rb[c, n, k] = finish(v)
-            for k in (1, 3, 2):
+            for k in (2, 1, 3):
                 send(rb.at[c, n, k], rb.at[c, n, 3 + k], r_send, r_recv.at[c], z_peer(4 - k))
 
     def output_stage(c):

time: 150 us -> 150 us (level)
  no operation moved by 1% of the time
where the time goes in v5:
time: 150 us
  Pallas kernels  148 us (99%)
  local copies, waits for them, and re-layouts  2.02 us (1%)
    pallas_call x1, Pallas kernels, per_device(): pl.pallas_call(functools.partial(kernel, chunks, rows), out_shape=pltpu.V...  148 us

profile of v5, /device:TPU:0, one launch (start us, length us, event | category | flops | bytes accessed | tf_op | source)
XLA Modules:
  0.0 149.9 jit_solution(17737735236709758025)
XLA Ops:
  0.0 147.9 %butterfly.1 = bf16[8192,256]{1,0:T(8,128)(2,1)S(1)} custom-call(bf16[8192,256]{1,0:T(8,128)(2,1)} %bitcast.3, bf16[4,8,256,256]{3,2,1,0:T(8,128)(2,1)} %sw_hbm.1, bf16[4,8,256,256]{3,2,1,0:T(8,128)(2,1)} %cw_hbm.1, f32[4,8,256]{2,1,0:T(8,128)} %lb_hbm.1, bf16[8,256,256]{2,1,0:T(8,128)(2,1)} %gw_hbm.1, f32[8,256]{1,0:T(8,128)} %gb_hbm.1), custom_call_target="tpu_custom_call" | custom-call | tf_op jit(solution)/shard_map/butterfly/pallas_call | solution.py:297
  147.9 2.0 %copy.8 = bf16[1024,8,256]{2,1,0:T(8,128)(2,1)} copy(bf16[1024,8,256]{2,1,0:T(8,128)(2,1)S(1)} %bitcast.2) | data formatting | bytes 8388608
